TPU v7x, 32 devices: a whole 2x2x4 slice. The times are simulated.
32 devices in a mesh: gy: 8 (over y, x, core), gx: 4 (over z).
Axes of the slice: x: 2, y: 2, z: 4, core: 2. Of those that a mesh axis runs over, the one named last changes fastest.
Arguments:
- fields: bfloat16 [16, 1472, 2048], P(None, 'gy', 'gx'), may hold values from -6 to 6
- level_order: int32 [16], replicated, may hold values from 0 to 15, each once
- m_owner: int32 [1024], replicated, may hold values from 0 to 7, as said below
- n_count: int32 [1024], replicated, may hold values from 1 to 736, as said below
Outputs:
- spectrum: float32 [16, 1536, 2944], P('gx', 'gy')
Inputs may be any that keep to these rules, and one draw needn't show every extreme that they name: `m_owner`: each owner is named by at most 192 wavenumbers m, and some owner by exactly 192. Wavenumbers n = 0 to n_count[m] - 1 are retained for m; the count for m = 0 is 736.
All inputs are finite; a program needn't handle non-finite values.
Results may differ from a plain program's by a relative error of at most 0.0066.
Values may be sent and summed in bfloat16 or wider, within the bound.
A program may use at most 64 MiB of HBM per device.

v0:
```python
import math

import jax
import jax.numpy as jnp
from jax import lax
from jax.sharding import PartitionSpec as P

NX = 2048
NY = 1472


def mode_tables(extent, mode_total):
    middle = extent // 2
    points = jnp.arange(middle + 1, dtype=jnp.int32)
    orders = jnp.arange(mode_total, dtype=jnp.int32)
    phases = (points[:, None] * orders[None, :] % extent).astype(jnp.float32) * (
        2.0 * math.pi / extent
    )
    weight = jnp.where((points == 0) | (points == middle), 0.5, 1.0).astype(jnp.float32)
    factor = 1.0 / math.sqrt(extent)
    cos_even = (weight[:, None] * jnp.cos(phases) * factor).astype(jnp.bfloat16)
    sin_odd = (-jnp.sin(phases) * factor).astype(jnp.bfloat16)
    return (cos_even, sin_odd)


def fold_ends(values, along_dim):
    extent = values.shape[along_dim]
    middle = extent // 2
    leading = lax.slice_in_dim(values, 0, middle + 1, axis=along_dim)
    anchor = lax.slice_in_dim(values, 0, 1, axis=along_dim)
    trailing = jnp.flip(lax.slice_in_dim(values, middle, extent, axis=along_dim), along_dim)
    mirror = jnp.concatenate([anchor, trailing], along_dim)
    even_part = (leading.astype(jnp.float32) + mirror.astype(jnp.float32)).astype(jnp.bfloat16)
    odd_part = (leading.astype(jnp.float32) - mirror.astype(jnp.float32)).astype(jnp.bfloat16)
    return (even_part, odd_part)


def slot_table(m_owner, groups, capacity):
    mode_count = m_owner.shape[0]
    modes = jnp.arange(mode_count, dtype=jnp.int32)
    keys = m_owner * mode_count + modes
    ordering = jnp.argsort(keys, stable=True)
    sorted_owner = jnp.take(m_owner, ordering)
    owners = jnp.arange(groups, dtype=jnp.int32)
    counts = jnp.sum((m_owner[:, None] == owners[None, :]).astype(jnp.int32), axis=0)
    starts = jnp.cumsum(counts) - counts
    within = modes - jnp.take(starts, sorted_owner)
    slot_index = sorted_owner * capacity + within
    slot_modes = jnp.zeros((groups * capacity,), jnp.int32).at[slot_index].set(ordering)
    filled = jnp.zeros((groups * capacity,), jnp.float32).at[slot_index].set(1.0)
    return (slot_modes, filled)


def body(fields, level_order, m_owner, n_count):
    groups_x = lax.axis_size("gx")
    groups_y = lax.axis_size("gy")
    per_set = fields.shape[0] // groups_x
    mode_count = m_owner.shape[0]
    wave_count = NY // 2
    capacity = 3 * mode_count // (2 * groups_y)
    ordered = jnp.take(fields, level_order, axis=0)
    line_data = lax.all_to_all(ordered, "gx", split_axis=0, concat_axis=2, tiled=True)
    cos_x, sin_x = mode_tables(NX, mode_count)
    even_part, odd_part = fold_ends(line_data, 2)
    along = jnp.einsum("lyx,xm->lym", even_part, cos_x, preferred_element_type=jnp.float32).astype(
        jnp.bfloat16
    )
    across = jnp.einsum("lyx,xm->lym", odd_part, sin_x, preferred_element_type=jnp.float32).astype(
        jnp.bfloat16
    )
    spectra = jnp.stack([along, across], 1)
    slot_modes, filled = slot_table(m_owner, groups_y, capacity)
    outgoing = jnp.take(spectra, slot_modes, axis=3)
    arrived = lax.all_to_all(outgoing, "gy", split_axis=3, concat_axis=2, tiled=True)
    first_slot = lax.axis_index("gy") * capacity
    own_modes = lax.dynamic_slice_in_dim(slot_modes, first_slot, capacity)
    own_filled = lax.dynamic_slice_in_dim(filled, first_slot, capacity)
    own_counts = jnp.take(n_count, own_modes)
    retained = (jnp.arange(wave_count, dtype=jnp.int32)[None, :] < own_counts[:, None]).astype(
        jnp.float32
    ) * own_filled[:, None]
    cos_y, sin_y = mode_tables(NY, wave_count)
    even_y, odd_y = fold_ends(arrived, 2)
    cosine_part = jnp.einsum("lcys,yn->lscn", even_y, cos_y, preferred_element_type=jnp.float32)
    sine_part = jnp.einsum("lcys,yn->lscn", odd_y, sin_y, preferred_element_type=jnp.float32)
    result = jnp.stack([cosine_part, sine_part], 3) * retained[None, :, None, None, :]
    return result.reshape(per_set, capacity, 4 * wave_count)


def solution(mesh):
    in_specs = (P(None, "gy", "gx"), P(), P(), P())
    out_specs = P("gx", "gy", None)
    return jax.shard_map(body, mesh=mesh, in_specs=in_specs, out_specs=out_specs, check_vma=False)
```

profile of v0, /device:TPU:0, one launch (start us, length us, event | category | flops | bytes accessed | tf_op | source)
XLA Modules:
  0.0 381.1 jit_solution(8535195543744656473)
XLA Ops:
  0.0 0.0 copy-start
  0.0 0.8 compare_select_fusion.5
  0.8 0.8 compare_and_fusion.1
  1.6 0.3 copy-done
  1.9 2.4 gather_fusion.1
  4.2 3.8 %broadcast_select_fusion = bf16[16,184,512]{2,1,0:T(8,128)(2,1)} fusion(bf16[16,184,512]{2,1,0:T(8,128)(2,1)} %gather_fusion.1, pred[16]{0:T(512)(128)(4,1)S(1)} %compare_and_fusion.1), kind=kLoop, calls=%fused_computation.31 | loop fusion | flops 1507328 | bytes 6029328 | tf_op jit(solution)/shard_map/jit(_take)/select_n | solution.py:61
  8.1 0.0 copy-start.2
  8.1 6.5 %all-to-all-start = ((bf16[16,184,512]{2,1,0:T(8,128)(2,1)}), bf16[16,184,512]{2,1,0:T(8,128)(2,1)}, u32[]{:S(2)}, u32[]{:S(2)}) async-start(bf16[16,184,512]{2,1,0:T(8,128)(2,1)} %broadcast_select_fusion), calls=%async_computation | async-start | bytes 6029312 | tf_op jit(solution)/shard_map/all_to_all | solution.py:62
  14.5 0.0 copy-done.2
  14.6 4.4 %sort.17 = (s32[1024]{0:T(1024)}, s32[1024]{0:T(1024)S(1)}) sort(s32[1024]{0:T(1024)S(1)} %iota_add_fusion, s32[1024]{0:T(1024)S(1)} %iota.45), dimensions={0}, to_apply=%region_0.1 | sort | flops 10240 | bytes 16384 | tf_op jit(solution)/shard_map/jit(argsort)/sort | solution.py:42
  18.9 4.5 %gather_fusion = s32[1024]{0:T(1024)S(1)} fusion(s32[1024]{0:T(1024)S(1)} %copy-done.2, s32[1024]{0:T(1024)S(1)} %fusion.89), kind=kCustom, calls=%fused_computation | custom fusion | bytes 12288 | tf_op jit(solution)/shard_map/jit(_take)/gather | solution.py:43
  23.4 0.1 convert_reduce_fusion
  23.6 0.2 reduce-window.9
  23.8 0.7 fusion.112
  24.4 5.1 %compare_select_fusion.1 = s32[1024]{0:T(1024)S(1)} fusion(s32[1024]{0:T(1024)S(1)} %gather_fusion, s32[1024]{0:T(1024)S(1)} %get-tuple-element.6, s32[]{:T(128)} %bitcast.4, s32[]{:T(128)} %bitcast.5, s32[]{:T(128)} %bitcast.6, s32[]{:T(128)} %bitcast.7, s32[]{:T(128)} %bitcast.8, s32[]{:T(128)} %bitcast.9, s32[]{:T(128)} %bitcast.10, s32[]{:T(128)} %bitcast.11), kind=kLoop, calls=%fused_computation.77 | loop fusion | flops 34816 | bytes 12320 | tf_op jit(solution)/shard_map/select_n | solution.py:49
  29.6 4.3 %scatter_custom_fusion = s32[1536]{0:T(1024)S(1)} fusion(s32[1024]{0:T(1024)S(1)} %compare_select_fusion.1, s32[1024]{0:T(1024)S(1)} %get-tuple-element.6, s32[]{:T(128)} %constant.71.clone.1), kind=kCustom, calls=%fused_computation.94 | custom fusion | bytes 6148 | tf_op jit(solution)/shard_map/scatter | solution.py:49
  34.0 48.5 %all-to-all-done = bf16[16,184,512]{2,1,0:T(8,128)(2,1)} async-done(((bf16[16,184,512]{2,1,0:T(8,128)(2,1)}), bf16[16,184,512]{2,1,0:T(8,128)(2,1)}, u32[]{:S(2)}, u32[]{:S(2)}) %all-to-all-start) | async-done | bytes 3014688 | tf_op jit(solution)/shard_map/all_to_all | solution.py:62
  82.5 2.3 copy.17
  84.8 1.3 slice.43
  86.2 31.8 %rev.8 = bf16[4,184,1024]{2,1,0:T(8,128)(2,1)} reverse(bf16[4,184,1024]{2,1,0:T(8,128)(2,1)} %slice.43), dimensions={2} | reverse | bytes 3014656 | tf_op jit(solution)/shard_map/jit(_flip)/rev | solution.py:31
  118.0 0.0 copy-start.4
  118.0 19.1 %fusion.57 = bf16[4,1,184,1024]{3,2,0,1:T(8,128)(2,1)S(1)} fusion(bf16[4,184,2048]{2,1,0:T(8,128)(2,1)S(1)} %bitcast.69, bf16[4,184,1024]{2,1,0:T(8,128)(2,1)} %rev.8, bf16[4,184,1]{2,1,0:T(8,128)(2,1)S(1)} %slice.42), kind=kOutput, calls=%fused_computation.60 | convolution fusion | flops 1568888832 | bytes 4898816 | tf_op jit(solution)/shard_map/lyx,xm->lym/dot_general | solution.py:68
  137.1 0.0 copy-done.4
  137.1 18.7 %fusion.52 = bf16[4,1,184,1024]{3,2,0,1:T(8,128)(2,1)S(1)} fusion(f32[1025]{0:T(1024)S(1)} %fusion.77, bf16[4,184,2048]{2,1,0:T(8,128)(2,1)S(1)} %bitcast.70, bf16[4,184,1024]{2,1,0:T(8,128)(2,1)S(1)} %copy-done.4, bf16[4,184,1]{2,1,0:T(8,128)(2,1)S(1)} %slice.42), kind=kOutput, calls=%fused_computation.59 | convolution fusion | flops 1568888832 | bytes 4907008 | tf_op jit(solution)/shard_map/lyx,xm->lym/dot_general | solution.py:65
  155.7 0.3 pad_maximum_fusion.1
  156.0 4.8 %copy.12 = bf16[4,2,184,1024]{2,0,3,1:T(4,128)(2,1)} copy(bf16[4,2,184,1024]{3,2,0,1:T(8,128)(2,1)S(1)} %pad_maximum_fusion.1) | data formatting | bytes 6029312 | tf_op jit(solution)/shard_map/stack | solution.py:71
  160.8 10.8 %gather_fusion.2 = bf16[1536,4,2,184]{3,1,2,0:T(4,128)(2,1)} fusion(bf16[4,2,184,1024]{2,0,3,1:T(4,128)(2,1)} %copy.12, s32[2048]{0:T(1024)S(1)} %pad_clamp_fusion), kind=kCustom, calls=%fused_computation.2 | custom fusion | bytes 9050112 | tf_op jit(solution)/shard_map/jit(_take)/gather | solution.py:73
  171.7 9.2 %select_bitcast_fusion = bf16[4,2,184,1536]{2,0,1,3:T(4,128)(2,1)} fusion(bf16[1536,4,2,184]{3,1,2,0:T(4,128)(2,1)} %gather_fusion.2, pred[1536]{0:T(1024)(128)(4,1)S(1)} %compare_and_fusion), kind=kLoop, calls=%fused_computation.11 | loop fusion | flops 2260992 | bytes 9045504 | tf_op jit(solution)/shard_map/jit(_take)/select_n | solution.py:73
  180.9 0.0 copy-start.3
  180.9 4.9 %all-to-all-start.1 = ((bf16[4,2,184,1536]{2,0,1,3:T(4,128)(2,1)}), bf16[4,2,184,1536]{2,0,1,3:T(4,128)(2,1)}, u32[]{:S(2)}, u32[]{:S(2)}) async-start(bf16[4,2,184,1536]{2,0,1,3:T(4,128)(2,1)} %select_bitcast_fusion), calls=%async_computation.1 | async-start | bytes 12582912 | tf_op jit(solution)/shard_map/all_to_all | solution.py:74
  185.8 4.3 %scatter_custom_fusion.1 = f32[1536]{0:T(1024)S(1)} fusion(s32[1024]{0:T(1024)S(1)} %compare_select_fusion.1, f32[1024]{0:T(1024)S(1)} %broadcast.138, f32[]{:T(128)} %constant.133.clone.1), kind=kCustom, calls=%fused_computation.91 | custom fusion | bytes 6148 | tf_op jit(solution)/shard_map/scatter | solution.py:50
  190.1 0.1 dynamic_slice.7
  190.2 0.1 compare_select_fusion.4
  190.3 0.0 copy-done.3
  190.3 1.2 gather_fusion.3
  191.5 0.1 and_select_fusion
  191.5 0.2 fusion.75
  191.7 0.6 mul.143
  192.3 3.7 mul.144
  196.1 61.3 %all-to-all-done.1 = bf16[4,2,184,1536]{2,0,1,3:T(4,128)(2,1)} async-done(((bf16[4,2,184,1536]{2,0,1,3:T(4,128)(2,1)}), bf16[4,2,184,1536]{2,0,1,3:T(4,128)(2,1)}, u32[]{:S(2)}, u32[]{:S(2)}) %all-to-all-start.1) | async-done | bytes 4522016 | tf_op jit(solution)/shard_map/all_to_all | solution.py:74
  257.3 9.1 %copy.19 = bf16[4,2,184,8,192]{2,3,4,1,0:T(8,128)(2,1)} copy(bf16[4,2,184,8,192]{2,0,1,4,3:T(4,128)(2,1)} %bitcast.19) | data formatting | bytes 9043968 | tf_op jit(solution)/shard_map/all_to_all | solution.py:74
  266.4 11.2 %all_to_all.33 = bf16[4,2,1472,192]{2,3,1,0:T(8,128)(2,1)} reshape(bf16[4,2,8,184,192]{3,2,4,1,0:T(8,128)(2,1)} %bitcast.63) | data formatting | bytes 9043968 | tf_op jit(solution)/shard_map/all_to_all | solution.py:74
  277.5 2.9 slice.46
  280.4 1.0 slice.45
  281.5 33.9 %reverse = bf16[4,2,768,192]{2,3,1,0:T(8,128)(2,1)} reverse(bf16[4,2,768,192]{2,3,1,0:T(8,128)(2,1)S(1)} %bitcast.66), dimensions={2} | reverse | bytes 4718592
  315.4 0.0 slice-start
  315.4 2.9 slice.67
  318.3 0.0 slice-start.1
  318.3 12.4 %fusion.17 = f32[4,192,2,1,736]{4,1,2,0,3:T(8,128)S(1)} fusion(bf16[4,2,1472,192]{2,3,1,0:T(8,128)(2,1)} %all_to_all.33, bf16[4,2,736,192]{2,3,1,0:T(8,128)(2,1)S(1)} %slice.67, bf16[4,2,1,192]{2,3,1,0:T(8,128)(2,1)S(1)} %slice.45), kind=kOutput, calls=%fused_computation.36 | convolution fusion | flops 1680784512 | bytes 9145344 | tf_op jit(solution)/shard_map/lcys,yn->lscn/dot_general | solution.py:85
  330.8 0.2 slice-done
  331.0 0.0 slice-done.1
  331.0 12.8 %fusion.14 = f32[4,192,2,1,736]{4,1,2,0,3:T(8,128)} fusion(bf16[4,2,1472,192]{2,3,1,0:T(8,128)(2,1)S(1)} %bitcast.65, bf16[4,2,736,192]{2,3,1,0:T(8,128)(2,1)S(1)} %slice.67, bf16[4,2,1,192]{2,3,1,0:T(8,128)(2,1)S(1)} %slice.45, f32[737]{0:T(1024)S(1)} %fusion.85), kind=kOutput, calls=%fused_computation.35 | convolution fusion | flops 1680784512 | bytes 9637888 | tf_op jit(solution)/shard_map/lcys,yn->lscn/dot_general | solution.py:84
  343.8 3.2 pad_maximum_fusion
  347.0 11.6 %copy.14 = f32[4,192,2,2,736]{4,3,2,1,0:T(2,128)} copy(f32[4,192,2,2,736]{4,1,2,0,3:T(8,128)S(1)} %pad_maximum_fusion) | data formatting | bytes 18087936 | tf_op jit(solution)/shard_map/stack | solution.py:86
  358.6 13.6 %stack.26 = f32[4,192,2944]{2,1,0:T(8,128)} reshape(f32[4,192,2,2,736]{4,3,2,1,0:T(2,128)} %copy.14) | data formatting | bytes 18087936 | tf_op jit(solution)/shard_map/stack | solution.py:86
  372.2 0.0 copy-start.1
  372.2 8.6 %broadcast_multiply_fusion = f32[4,192,2944]{2,1,0:T(8,128)} fusion(f32[4,192,2944]{2,1,0:T(8,128)} %stack.26, f32[192,2944]{1,0:T(8,128)} %mul.144), kind=kLoop, calls=%fused_computation.16 | loop fusion | flops 2260992 | bytes 20348928 | tf_op jit(solution)/shard_map/mul | solution.py:86
  380.9 0.0 copy-done.1
  (14 shorter events, 0.1 us)
Async XLA Ops:
  0.0 1.9 copy-start
  8.1 6.5 %copy-start.2 = (s32[1024]{0:T(1024)S(1)}, s32[1024]{0:T(1024)}, u32[]{:S(2)}) copy-start(s32[1024]{0:T(1024)} %param.6) | copy-start | bytes 12292
  8.1 74.4 %all-to-all-start = ((bf16[16,184,512]{2,1,0:T(8,128)(2,1)}), bf16[16,184,512]{2,1,0:T(8,128)(2,1)}, u32[]{:S(2)}, u32[]{:S(2)}) async-start(bf16[16,184,512]{2,1,0:T(8,128)(2,1)} %broadcast_select_fusion), calls=%async_computation | async-start | bytes 6029312 | tf_op jit(solution)/shard_map/all_to_all | solution.py:62
  118.0 19.1 %copy-start.4 = (bf16[4,184,1024]{2,1,0:T(8,128)(2,1)S(1)}, bf16[4,184,1024]{2,1,0:T(8,128)(2,1)}, u32[]{:S(2)}) copy-start(bf16[4,184,1024]{2,1,0:T(8,128)(2,1)} %rev.8) | copy-start | bytes 4521988
  180.9 9.4 %copy-start.3 = (s32[1024]{0:T(1024)S(1)}, s32[1024]{0:T(1024)}, u32[]{:S(2)}) copy-start(s32[1024]{0:T(1024)} %param.7) | copy-start | bytes 12292
  180.9 76.4 %all-to-all-start.1 = ((bf16[4,2,184,1536]{2,0,1,3:T(4,128)(2,1)}), bf16[4,2,184,1536]{2,0,1,3:T(4,128)(2,1)}, u32[]{:S(2)}, u32[]{:S(2)}) async-start(bf16[4,2,184,1536]{2,0,1,3:T(4,128)(2,1)} %select_bitcast_fusion), calls=%async_computation.1 | async-start | bytes 12582912 | tf_op jit(solution)/shard_map/all_to_all | solution.py:74
  315.4 15.6 %slice-start = ((s8[4718592]{0:T(1024)(128)(4,1)}), s8[4194304]{0:T(1024)(128)(4,1)S(1)}, s32[]{:S(2)}) async-start(s8[4718592]{0:T(1024)(128)(4,1)} %bitcast.64), calls=%async_computation.2 | async-start | bytes 8388608
  318.3 12.6 %slice-start.1 = ((s8[4718592]{0:T(1024)(128)(4,1)}), s8[524288]{0:T(1024)(128)(4,1)S(1)}, s32[]{:S(2)}) async-start(s8[4718592]{0:T(1024)(128)(4,1)} %bitcast.64), calls=%async_computation.3 | async-start | bytes 1048576
  372.2 8.6 %copy-start.1 = (bf16[16,184,512]{2,1,0:T(8,128)(2,1)S(1)}, bf16[16,184,512]{2,1,0:T(8,128)(2,1)}, u32[]{:S(2)}) copy-start(bf16[16,184,512]{2,1,0:T(8,128)(2,1)} %param.4) | copy-start | bytes 9043972
where the time goes:
time: 388 us; the launch traced here: 381 us
  local copies, waits for them, and re-layouts  160 us (41%)
  waiting for transfers between devices  110 us (28%)
  matrix products  63 us (16%)
  other arithmetic  36.9 us (10%)
  starting transfers between devices  11.3 us (3%)
    all_to_all x1, waiting for transfers between devices, body(): lax.all_to_all(outgoing, 'gy', split_axis=3, concat_axis=2, tiled=True)  61.3 us
    all_to_all x1, waiting for transfers between devices, body(): lax.all_to_all(ordered, 'gx', split_axis=0, concat_axis=2, tiled=True)  48.5 us
    unnamed x16, local copies, waits for them, and re-layouts  37.3 us
    rev x1, local copies, waits for them, and re-layouts, fold_ends(): jnp.flip(lax.slice_in_dim(values, middle, extent, axis=along_dim), along_...  31.8 us
    another operation x2, local copies, waits for them, and re-layouts, body(): jnp.stack([cosine_part, sine_part], 3) * retained[None, :, None, None, :]  25.2 us
    all_to_all x2, local copies, waits for them, and re-layouts, body(): lax.all_to_all(outgoing, 'gy', split_axis=3, concat_axis=2, tiled=True)  20.2 us
    dot_general x1, matrix products, body(): jnp.einsum('lyx,xm->lym', odd_part, sin_x, preferred_element_type=jnp.flo...  19.1 us
    dot_general x1, matrix products, body(): jnp.einsum('lyx,xm->lym', even_part, cos_x, preferred_element_type=jnp.fl...  18.7 us
  transfers between devices with their start and end apart: 2, of which 2 were waited for; matrix products, arithmetic and copies ran while one was open for 8% of the time, Pallas kernels for 0%

commit v1 on v0

--- a/solution.py
+++ b/solution.py
@@ -1,12 +1,19 @@
+import functools
 import math
 
 import jax
+import ml_dtypes
+import numpy as np
 import jax.numpy as jnp
 from jax import lax
+from jax.experimental import pallas as pl
+from jax.experimental.pallas import tpu as pltpu
 from jax.sharding import PartitionSpec as P
 
 NX = 2048
 NY = 1472
+MESH = pl.DeviceIdType.MESH
+COARSE = 32
 
 
 def mode_tables(extent, mode_total):
@@ -87,7 +94,264 @@
     return result.reshape(per_set, capacity, 4 * wave_count)
 
 
+def unit_angles(products, extent):
+    phases = (products % extent).astype(np.float64) * (2.0 * math.pi / extent)
+    cosine = np.cos(phases)
+    sine = np.where((products * 2) % extent == 0, 0.0, np.sin(phases))
+    return cosine, sine
+
+
+def split_x_table(extent, mode_total):
+    modes = np.arange(mode_total)
+    coarse = np.arange(extent // COARSE)[:, None] * COARSE * modes[None, :]
+    fine = np.arange(COARSE)[:, None] * modes[None, :]
+    cos_a, sin_a = unit_angles(coarse, extent)
+    cos_b, sin_b = unit_angles(fine, extent)
+    factor = 1.0 / math.sqrt(extent)
+    rest = np.concatenate([cos_a * factor, sin_a * factor, cos_b, sin_b], 0).astype(np.float32)
+    terms = []
+    for _ in range(3):
+        term = rest.astype(ml_dtypes.bfloat16)
+        terms.append(term)
+        rest = rest - term.astype(np.float32)
+    return np.stack(terms, 0)
+
+
+def full_y_table(extent, wave_total):
+    points = np.arange(extent)[:, None]
+    orders = np.arange(wave_total)[None, :]
+    cosine, sine = unit_angles(points * orders, extent)
+    factor = 1.0 / math.sqrt(extent)
+    both = np.concatenate([cosine * factor, -sine * factor], 1).astype(np.float32)
+    return both.astype(ml_dtypes.bfloat16)
+
+
+def exchange_kernel(
+    groups_x, groups_y, capacity, order_ref, fields_ref, owner_row_ref, owner_col_ref, count_ref,
+    split_ref, out_ref, keep_ref, send_x, line, slot_col, parts, table, spectra,
+    x_send_sem, x_recv_sem, y_send_sem, y_recv_sem, own_sem,
+):
+    me_x = lax.axis_index("gx")
+    me_y = lax.axis_index("gy")
+    levels, rows, width = fields_ref.shape
+    per_set = levels // groups_x
+    mode_count = owner_row_ref.shape[1]
+    pair = 2 * capacity
+    coarse_total = groups_x * width // COARSE
+
+    barrier = pltpu.get_barrier_semaphore()
+    for step in range(1, groups_x):
+        pl.semaphore_signal(
+            barrier, inc=1, device_id={"gx": lax.rem(me_x + step, groups_x)}, device_id_type=MESH
+        )
+    for step in range(1, groups_y):
+        pl.semaphore_signal(
+            barrier, inc=1, device_id={"gy": lax.rem(me_y + step, groups_y)}, device_id_type=MESH
+        )
+
+    def x_copy(chunk, step):
+        peer = lax.rem(me_x + step, groups_x)
+        return pltpu.make_async_remote_copy(
+            src_ref=send_x.at[chunk, peer],
+            dst_ref=line.at[chunk, me_x],
+            send_sem=x_send_sem.at[chunk, step],
+            recv_sem=x_recv_sem.at[chunk, step],
+            device_id={"gx": peer},
+            device_id_type=MESH,
+        )
+
+    def y_copy(chunk, step):
+        peer = lax.rem(me_y + step, groups_y)
+        return pltpu.make_async_remote_copy(
+            src_ref=spectra.at[chunk, peer],
+            dst_ref=out_ref.at[chunk, me_y],
+            send_sem=y_send_sem.at[chunk, step],
+            recv_sem=y_recv_sem.at[chunk, step],
+            device_id={"gy": peer},
+            device_id_type=MESH,
+        )
+
+    for chunk in range(per_set):
+        for group in range(groups_x):
+            send_x[chunk, group] = fields_ref[order_ref[group * per_set + chunk]]
+        line[chunk, me_x] = fields_ref[order_ref[me_x * per_set + chunk]]
+        if chunk == 0:
+            pl.semaphore_wait(barrier, groups_x + groups_y - 2)
+        for step in range(1, groups_x):
+            x_copy(chunk, step).start()
+
+    row_block = 128
+    def rank_block(block, carry):
+        start = pl.multiple_of(block * row_block, row_block)
+        own = owner_col_ref[pl.ds(start, row_block), :]
+        before = lax.broadcasted_iota(jnp.int32, (row_block, mode_count), 1)
+        here = lax.broadcasted_iota(jnp.int32, (row_block, mode_count), 0) + start
+        same = jnp.where((owner_row_ref[...] == own) & (before < here), 1.0, 0.0)
+        rank = jnp.sum(same, axis=1, keepdims=True).astype(jnp.int32)
+        slot_col[pl.ds(start, row_block), :] = own * capacity + rank
+        return carry
+
+    lax.fori_loop(0, mode_count // row_block, rank_block, 0)
+
+    def picked(first, size):
+        lane = lax.broadcasted_iota(jnp.int32, (mode_count, size), 1)
+        target = first + jnp.where(lane < capacity, lane, lane - capacity)
+        return jnp.where(slot_col[...] == target, 1.0, 0.0).astype(jnp.bfloat16)
+
+    own_pick = picked(me_y * capacity, pair)
+    kept = lax.dot_general(
+        own_pick, count_ref[...], (((0,), (0,)), ((), ())), preferred_element_type=jnp.float32
+    )
+    keep_ref[...] = kept[:capacity]
+
+    def table_of(owner, carry):
+        pick = picked(owner * capacity, pair)
+        small = jnp.dot(split_ref[0], pick, preferred_element_type=jnp.float32)
+        small += jnp.dot(split_ref[1], pick, preferred_element_type=jnp.float32)
+        small += jnp.dot(split_ref[2], pick, preferred_element_type=jnp.float32)
+        cos_a = small[:coarse_total]
+        sin_a = small[coarse_total : 2 * coarse_total]
+        lane = lax.broadcasted_iota(jnp.int32, (coarse_total, pair), 1)
+        parts[0] = jnp.where(lane < capacity, cos_a, -sin_a)
+        parts[1] = jnp.where(lane < capacity, -sin_a, -cos_a)
+        cos_b = small[2 * coarse_total : 2 * coarse_total + COARSE]
+        sin_b = small[2 * coarse_total + COARSE :]
+
+        def fill(a, inner):
+            value = parts[0, pl.ds(a, 1), :] * cos_b + parts[1, pl.ds(a, 1), :] * sin_b
+            start = pl.multiple_of(a * COARSE, COARSE)
+            table[owner, pl.ds(start, COARSE), :] = value.astype(jnp.bfloat16)
+            return inner
+
+        lax.fori_loop(0, coarse_total, fill, 0)
+        return carry
+
+    lax.fori_loop(0, groups_y, table_of, 0)
+
+    for chunk in range(per_set):
+        for step in range(1, groups_x):
+            x_copy(chunk, step).wait_recv()
+
+        def transform(owner, carry):
+            whole = jnp.concatenate([line[chunk, g] for g in range(groups_x)], axis=1)
+            value = jnp.dot(whole, table[owner], preferred_element_type=jnp.float32)
+            spectra[chunk, owner] = value.astype(jnp.bfloat16)
+            return carry
+
+        lax.fori_loop(0, groups_y, transform, 0)
+        for step in range(1, groups_y):
+            y_copy(chunk, step).start()
+        pltpu.make_async_copy(
+            spectra.at[chunk, me_y], out_ref.at[chunk, me_y], own_sem.at[chunk]
+        ).start()
+
+    for chunk in range(per_set):
+        for step in range(1, groups_x):
+            x_copy(chunk, step).wait_send()
+        for step in range(1, groups_y):
+            y_copy(chunk, step).wait()
+        pltpu.make_async_copy(
+            spectra.at[chunk, me_y], out_ref.at[chunk, me_y], own_sem.at[chunk]
+        ).wait()
+
+
+def wave_kernel(capacity, wave_count, spectra_ref, first_ref, second_ref, keep_ref, out_ref):
+    turned = spectra_ref[0].T
+    total = 4 * wave_count
+    span = first_ref.shape[1]
+    keep = keep_ref[:, 0:1]
+
+    def kept(value, start):
+        column = lax.broadcasted_iota(jnp.int32, value.shape, 1) + start
+        order = column
+        for part in range(1, 4):
+            order = jnp.where(column >= part * wave_count, column - part * wave_count, order)
+        return jnp.where(order.astype(jnp.float32) < keep, value, 0.0)
+
+    low = jnp.dot(turned[:capacity], first_ref[...], preferred_element_type=jnp.float32)
+    high = jnp.dot(turned[capacity:], second_ref[...], preferred_element_type=jnp.float32)
+    edge = total - span
+    out_ref[0, :, :edge] = kept(low[:, :edge], 0)
+    out_ref[0, :, edge:span] = kept(low[:, edge:] + high[:, : span - edge], edge)
+    out_ref[0, :, span:] = kept(high[:, span - edge :], span)
+
+
+def fused_body(groups_x, groups_y, fields, level_order, m_owner, n_count):
+    levels, rows, width = fields.shape
+    per_set = levels // groups_x
+    mode_count = m_owner.shape[0]
+    wave_count = NY // 2
+    capacity = 3 * mode_count // (2 * groups_y)
+    pair = 2 * capacity
+    extent_x = width * groups_x
+    extent_y = rows * groups_y
+    split = jnp.asarray(split_x_table(extent_x, mode_count))
+    y_table = full_y_table(extent_y, wave_count)
+    span = -(-(2 * wave_count) // 128) * 128
+    gap = span - 2 * wave_count
+    first = jnp.asarray(np.pad(y_table, ((0, 0), (0, gap))))
+    second = jnp.asarray(np.pad(y_table, ((0, 0), (gap, 0))))
+    counts = n_count.astype(jnp.int32)[:, None]
+    lanes = lax.broadcasted_iota(jnp.int32, (mode_count, 128), 1)
+    count_parts = jnp.where(
+        lanes < 64, jnp.where(lanes == 0, counts // 8 * 8, 0), jnp.where(lanes == 64, counts % 8, 0)
+    ).astype(jnp.bfloat16)
+    vmem = pl.BlockSpec(memory_space=pltpu.VMEM)
+    smem = pl.BlockSpec(memory_space=pltpu.SMEM)
+    arrived, keep = pl.pallas_call(
+        functools.partial(exchange_kernel, groups_x, groups_y, capacity),
+        out_shape=(
+            jax.ShapeDtypeStruct((per_set, groups_y, rows, pair), jnp.bfloat16),
+            jax.ShapeDtypeStruct((capacity, 128), jnp.float32),
+        ),
+        in_specs=[smem, vmem, vmem, vmem, vmem, vmem],
+        out_specs=(pl.BlockSpec(memory_space=pl.ANY), vmem),
+        scratch_shapes=[
+            pltpu.VMEM((per_set, groups_x, rows, width), jnp.bfloat16),
+            pltpu.VMEM((per_set, groups_x, rows, width), jnp.bfloat16),
+            pltpu.VMEM((mode_count, 1), jnp.int32),
+            pltpu.VMEM((2, extent_x // COARSE, pair), jnp.float32),
+            pltpu.VMEM((groups_y, extent_x, pair), jnp.bfloat16),
+            pltpu.VMEM((per_set, groups_y, rows, pair), jnp.bfloat16),
+            pltpu.SemaphoreType.DMA((per_set, groups_x)),
+            pltpu.SemaphoreType.DMA((per_set, groups_x)),
+            pltpu.SemaphoreType.DMA((per_set, groups_y)),
+            pltpu.SemaphoreType.DMA((per_set, groups_y)),
+            pltpu.SemaphoreType.DMA((per_set,)),
+        ],
+        compiler_params=pltpu.CompilerParams(
+            collective_id=0, has_side_effects=True, vmem_limit_bytes=60 * 1024 * 1024
+        ),
+        name="exchange",
+    )(level_order, fields, m_owner[None, :], m_owner[:, None], count_parts, split)
+    keep = keep[:, :1] + keep[:, 64:65]
+    keep = jnp.broadcast_to(keep, (capacity, 128))
+    return pl.pallas_call(
+        functools.partial(wave_kernel, capacity, wave_count),
+        grid=(per_set,),
+        out_shape=jax.ShapeDtypeStruct((per_set, capacity, 4 * wave_count), jnp.float32),
+        in_specs=[
+            pl.BlockSpec((1, extent_y, pair), lambda i: (i, 0, 0)),
+            pl.BlockSpec((extent_y, span), lambda i: (0, 0)),
+            pl.BlockSpec((extent_y, span), lambda i: (0, 0)),
+            pl.BlockSpec((capacity, 128), lambda i: (0, 0)),
+        ],
+        out_specs=pl.BlockSpec((1, capacity, 4 * wave_count), lambda i: (i, 0, 0)),
+        compiler_params=pltpu.CompilerParams(vmem_limit_bytes=60 * 1024 * 1024),
+        name="waves",
+    )(arrived.reshape(per_set, extent_y, pair), first, second, keep)
+
+
 def solution(mesh):
+    groups_x, groups_y = mesh.shape["gx"], mesh.shape["gy"]
     in_specs = (P(None, "gy", "gx"), P(), P(), P())
     out_specs = P("gx", "gy", None)
-    return jax.shard_map(body, mesh=mesh, in_specs=in_specs, out_specs=out_specs, check_vma=False)
+
+    def whole(fields, level_order, m_owner, n_count):
+        levels, rows, width = fields.shape
+        capacity = 3 * m_owner.shape[0] // (2 * groups_y)
+        if rows % 8 == 0 and width % 128 == 0 and capacity % 64 == 0 and levels % groups_x == 0:
+            return fused_body(groups_x, groups_y, fields, level_order, m_owner, n_count)
+        return body(fields, level_order, m_owner, n_count)
+
+    return jax.shard_map(whole, mesh=mesh, in_specs=in_specs, out_specs=out_specs, check_vma=False)

time: 388 us -> 119 us (0.31)
  the two profiles are of different devices: /device:TPU:0 before, /device:TPU:15 now
where the time goes in v1:
time: 119 us
  Pallas kernels  113 us (95%)
  other arithmetic  2.92 us (2%)
  local copies, waits for them, and re-layouts  2.45 us (2%)
    pallas_call x1, Pallas kernels, fused_body(): pl.pallas_call(functools.partial(exchange_kernel, groups_x, groups_y, cap...  99.5 us
    pallas_call x1, Pallas kernels, fused_body(): pl.pallas_call(functools.partial(wave_kernel, capacity, wave_count), grid...  13.6 us

profile of v1, /device:TPU:15, one launch (start us, length us, event | category | flops | bytes accessed | tf_op | source)
XLA Modules:
  0.0 118.6 jit_solution(8006340991564975460)
XLA Ops:
  0.0 0.7 fusion
  0.7 1.1 select_convert_fusion.count_ref
  1.8 1.7 %copy.8.owner_col_ref = s32[1024,1]{1,0:T(8,128)} copy(s32[1024,1]{0,1:T(1,128)} %bitcast.4) | data formatting | bytes 8192 | tf_op jit(solution)/shard_map/broadcast_in_dim | solution.py:326
  3.5 99.5 %exchange.1 = (bf16[4,8,184,384]{3,2,1,0:T(8,128)(2,1)}, f32[192,128]{1,0:T(8,128)}) custom-call(s32[16]{0:T(128)} %order_ref.1, bf16[16,184,512]{2,1,0:T(8,128)(2,1)} %fields_ref.1, s32[1,1024]{1,0:T(1,128)} %bitcast.5, s32[1024,1]{1,0:T(8,128)} %copy.8.owner_col_ref, bf16[1024,128]{1,0:T(8,128)(2,1)} %select_convert_fusion.count_ref, ...), custom_call_target="tpu_custom_call" | custom-call | tf_op jit(solution)/shard_map/exchange/pallas_call | solution.py:301
  103.0 1.1 add_reduce_fusion
  104.2 0.7 broadcast_in_dim.35.keep_ref
  104.9 13.6 %waves.1 = f32[4,192,2944]{2,1,0:T(8,128)} custom-call(bf16[4,1472,384]{2,1,0:T(8,128)(2,1)} %bitcast.3, bf16[1472,1536]{1,0:T(8,128)(2,1)} %constant.40.clone.first_ref, bf16[1472,1536]{1,0:T(8,128)(2,1)} %constant.41.clone.second_ref, f32[192,128]{1,0:T(8,128)} %broadcast_in_dim.35.keep_ref), custom_call_target="tpu_custom_call" | custom-call | tf_op jit(solution)/shard_map/waves/pallas_call | solution.py:329
  (2 shorter events, 0.0 us)
